TPU v7x, 32 devices: a whole 2x2x4 slice. The times are simulated.
32 devices in a mesh: wide: 8 (over y, x, core), narrow: 4 (over z).
Axes of the slice: x: 2, y: 2, z: 4, core: 2. Of those that a mesh axis runs over, the one named last changes fastest.
Arguments:
- layer_input: bfloat16 [2, 8, 256, 2048], P(None, 'wide', 'narrow'), may hold values from -6 to 6
- document_lengths: int32 [2, 8, 4], P(None, 'wide'), may hold values from 1 to 128, 256 in all within a row
- attn_gain: bfloat16 [2048], replicated, may hold values from 0.5 to 1.5
- w_query: bfloat16 [2048, 2048], P(None, 'narrow'), may hold values from -0.125 to 0.125
- w_key: bfloat16 [2048, 1024], P(None, 'narrow'), may hold values from -0.125 to 0.125
- w_value: bfloat16 [2048, 1024], P(None, 'narrow'), may hold values from -0.125 to 0.125
- query_gain: bfloat16 [128], replicated, may hold values from 1 to 2.5
- key_gain: bfloat16 [128], replicated, may hold values from 1 to 2.5
- w_out: bfloat16 [2048, 2048], P('narrow'), may hold values from -0.75 to 0.75
- mlp_gain: bfloat16 [2048], replicated, may hold values from 0.5 to 1.5
- w_gate: bfloat16 [2048, 6144], P(None, 'narrow'), may hold values from -0.125 to 0.125
- w_up: bfloat16 [2048, 6144], P(None, 'narrow'), may hold values from -0.125 to 0.125
- w_down: bfloat16 [6144, 2048], P('narrow'), may hold values from -0.078125 to 0.078125
- output_cotangent: bfloat16 [2, 8, 256, 2048], P(None, 'wide', 'narrow'), may hold values from -6 to 6
Outputs:
- layer_out: float32 [2, 8, 256, 2048], P(None, 'wide', 'narrow')
- in_grad: float32 [2, 8, 256, 2048], P(None, 'wide', 'narrow')
- attn_gain_grad: float32 [2048], replicated
- w_query_grad: float32 [2048, 2048], P('wide', 'narrow')
- w_key_grad: float32 [2048, 1024], P('wide', 'narrow')
- w_value_grad: float32 [2048, 1024], P('wide', 'narrow')
- query_gain_grad: float32 [128], replicated
- key_gain_grad: float32 [128], replicated
- w_out_grad: float32 [2048, 2048], P('narrow', 'wide')
- mlp_gain_grad: float32 [2048], replicated
- w_gate_grad: float32 [2048, 6144], P('wide', 'narrow')
- w_up_grad: float32 [2048, 6144], P('wide', 'narrow')
- w_down_grad: float32 [6144, 2048], P('narrow', 'wide')
Inputs may be any that keep to these rules, and one draw needn't show every extreme that they name: `document_lengths`: each row's 4 document lengths sum to 256, and in every row the longest is exactly 128.
All inputs are finite; a program needn't handle non-finite values.
Results may differ from a plain program's by a relative error of at most 0.013.
The roundings to bfloat16 on the way count: a program that leaves them out, or rounds other values in their place, can miss the bound.
Values may be sent and summed in bfloat16 or wider, within the bound.
A program may use at most 192 MiB of HBM per device.

v0:
```python
import jax
import jax.numpy as jnp
from jax import lax
from jax.sharding import PartitionSpec as P

norm_eps = 1e-06
masked_score = -1e30


def rms_scale(values):
    return lax.rsqrt(jnp.mean(values * values, axis=-1, keepdims=True) + norm_eps)


def rms_back(grad_in, normed_hat, scale_rows):
    return scale_rows * (
        grad_in - normed_hat * jnp.mean(grad_in * normed_hat, axis=-1, keepdims=True)
    )


def doc_layout(lengths, seq_len):
    doc_ends = jnp.cumsum(lengths)
    starts = doc_ends - lengths
    places = lax.iota(jnp.int32, seq_len)
    segment = jnp.sum((places[:, None] >= doc_ends[None, :]).astype(jnp.int32), axis=1)
    member = segment[:, None] == lax.iota(jnp.int32, lengths.shape[0])[None, :]
    doc_first = jnp.sum(jnp.where(member, starts[None, :], 0), axis=1)
    allowed = (segment[:, None] == segment[None, :]) & (places[None, :] <= places[:, None])
    return (places - doc_first, allowed)


def rope_tables(inside, head_dim):
    half_dim = head_dim // 2
    frequency = jnp.power(1000000.0, -2.0 * lax.iota(jnp.float32, half_dim) / head_dim)
    angles = inside.astype(jnp.float32)[:, None] * frequency[None, :]
    return (jnp.cos(angles), jnp.sin(angles))


def rotate(values, cos_table, sine_table):
    half_dim = values.shape[-1] // 2
    first_half = values[..., :half_dim]
    second = values[..., half_dim:]
    cos_wide = cos_table[:, None, :]
    sine_wide = sine_table[:, None, :]
    return jnp.concatenate(
        [first_half * cos_wide - second * sine_wide, second * cos_wide + first_half * sine_wide],
        axis=-1,
    )


def contract_rows(left_side, right_side):
    return lax.dot_general(
        left_side, right_side, (((0,), (0,)), ((), ())), preferred_element_type=jnp.float32
    )


def contract_cols(left_side, right_side):
    return lax.dot_general(
        left_side, right_side, (((1,), (1,)), ((), ())), preferred_element_type=jnp.float32
    )


def row_product(source, weight):
    return jnp.dot(source, weight, preferred_element_type=jnp.float32)


def row_back_product(source, weight):
    return contract_cols(source, weight)


def attention_scores(grouped, key_rot, allowed, score_scale):
    raw_scores = (
        jnp.einsum("tkgd,ukd->kgtu", grouped, key_rot, preferred_element_type=jnp.float32)
        * score_scale
    )
    return jnp.where(allowed[None, None], raw_scores, masked_score)


def local(
    layer_input,
    document_lengths,
    attn_gain,
    w_query,
    w_key,
    w_value,
    query_gain,
    key_gain,
    w_out,
    mlp_gain,
    w_gate,
    w_up,
    w_down,
    output_cotangent,
):
    shard_rows = layer_input.shape[2]
    seq_len = shard_rows * lax.axis_size("narrow")
    head_dim = query_gain.shape[0]
    query_cols = w_query.shape[1]
    key_cols = w_key.shape[1]
    query_heads = query_cols // head_dim
    kv_local = key_cols // head_dim
    group_size = query_cols // key_cols
    ff_cols = w_gate.shape[1]
    score_scale = head_dim ** (-0.5)
    w_qkv = jnp.concatenate([w_query, w_key, w_value], axis=1)
    w_both = jnp.concatenate([w_gate, w_up], axis=1)
    attn_gain_f = attn_gain.astype(jnp.float32)
    query_gain_f = query_gain.astype(jnp.float32)
    key_gain_f = key_gain.astype(jnp.float32)
    mlp_gain_f = mlp_gain.astype(jnp.float32)
    totals = None
    small_totals = None
    outputs_list = []
    in_grads = []
    for micro_step in range(layer_input.shape[0]):
        rows_in = layer_input[micro_step, 0].astype(jnp.float32)
        inside, allowed = doc_layout(document_lengths[micro_step, 0], seq_len)
        cos_table, sine_table = rope_tables(inside, head_dim)
        scale_one = rms_scale(rows_in)
        hat_one = rows_in * scale_one
        normed = (hat_one * attn_gain_f).astype(jnp.bfloat16)
        normed_full = lax.all_gather(normed, "narrow", axis=0, tiled=True)
        projected = jnp.dot(normed_full, w_qkv, preferred_element_type=jnp.float32)
        query_raw = projected[:, :query_cols].reshape(seq_len, query_heads, head_dim)
        key_raw = projected[:, query_cols : query_cols + key_cols].reshape(
            seq_len, kv_local, head_dim
        )
        value_rows = (
            projected[:, query_cols + key_cols :]
            .astype(jnp.bfloat16)
            .reshape(seq_len, kv_local, head_dim)
        )
        query_scale = rms_scale(query_raw)
        query_hat = query_raw * query_scale
        query_rot = rotate(query_hat * query_gain_f, cos_table, sine_table).astype(jnp.bfloat16)
        key_scale = rms_scale(key_raw)
        key_hat = key_raw * key_scale
        key_rot = rotate(key_hat * key_gain_f, cos_table, sine_table).astype(jnp.bfloat16)
        grouped = query_rot.reshape(seq_len, kv_local, group_size, head_dim)
        scores = attention_scores(grouped, key_rot, allowed, score_scale)
        top_score = jnp.max(scores, axis=-1, keepdims=True)
        exponent = jnp.exp(scores - top_score)
        total_mass = jnp.sum(exponent, axis=-1, keepdims=True)
        log_mass = top_score + jnp.log(total_mass)
        prob_low = (exponent / total_mass).astype(jnp.bfloat16)
        attn_mix = jnp.einsum(
            "kgtu,ukd->tkgd", prob_low, value_rows, preferred_element_type=jnp.float32
        )
        attn_mix = attn_mix.reshape(seq_len, query_cols).astype(jnp.bfloat16)
        attn_branch = lax.psum_scatter(
            row_product(attn_mix, w_out), "narrow", scatter_dimension=0, tiled=True
        )
        middle = rows_in + attn_branch
        scale_two = rms_scale(middle)
        hat_two = middle * scale_two
        normed_two = (hat_two * mlp_gain_f).astype(jnp.bfloat16)
        normed_two_full = lax.all_gather(normed_two, "narrow", axis=0, tiled=True)
        gate_up = jnp.dot(normed_two_full, w_both, preferred_element_type=jnp.float32)
        gate_pre = gate_up[:, :ff_cols]
        up_proj = gate_up[:, ff_cols:]
        sigmoid_gate = jax.nn.sigmoid(gate_pre)
        silu_gate = gate_pre * sigmoid_gate
        activated = (silu_gate * up_proj).astype(jnp.bfloat16)
        mlp_branch = lax.psum_scatter(
            row_product(activated, w_down).astype(jnp.bfloat16),
            "narrow",
            scatter_dimension=0,
            tiled=True,
        ).astype(jnp.float32)
        outputs_list.append(middle + mlp_branch)
        cot_rows = output_cotangent[micro_step, 0]
        cot_full = lax.all_gather(cot_rows, "narrow", axis=0, tiled=True)
        grad_down = contract_rows(activated, cot_full)
        d_act = contract_cols(cot_full, w_down)
        d_gate = d_act * up_proj * sigmoid_gate * (1.0 + gate_pre * (1.0 - sigmoid_gate))
        d_up = d_act * silu_gate
        d_both = jnp.concatenate([d_gate, d_up], axis=1).astype(jnp.bfloat16)
        grad_both = contract_rows(normed_two_full, d_both)
        d_normed_two = lax.psum_scatter(
            row_back_product(d_both, w_both), "narrow", scatter_dimension=0, tiled=True
        )
        mlp_gain_part = jnp.sum(d_normed_two * hat_two, axis=0)
        d_middle = cot_rows.astype(jnp.float32) + rms_back(
            d_normed_two * mlp_gain_f, hat_two, scale_two
        )
        d_branch = d_middle.astype(jnp.bfloat16)
        d_branch_full = lax.all_gather(d_branch, "narrow", axis=0, tiled=True)
        grad_out = contract_rows(attn_mix, d_branch_full)
        d_mix = contract_cols(d_branch_full, w_out).astype(jnp.bfloat16)
        d_mix = d_mix.reshape(seq_len, kv_local, group_size, head_dim)
        d_prob = jnp.einsum("tkgd,ukd->kgtu", d_mix, value_rows, preferred_element_type=jnp.float32)
        scores_again = attention_scores(grouped, key_rot, allowed, score_scale)
        prob_again = jnp.exp(scores_again - log_mass)
        prob_back_low = prob_again.astype(jnp.bfloat16)
        d_value = jnp.einsum(
            "kgtu,tkgd->ukd", prob_back_low, d_mix, preferred_element_type=jnp.float32
        )
        d_score = prob_again * (d_prob - jnp.sum(prob_again * d_prob, axis=-1, keepdims=True))
        d_score = d_score.astype(jnp.bfloat16)
        d_query = jnp.einsum("kgtu,ukd->tkgd", d_score, key_rot, preferred_element_type=jnp.float32)
        d_query = d_query.reshape(seq_len, query_heads, head_dim) * score_scale
        d_key = (
            jnp.einsum("kgtu,tkgd->ukd", d_score, grouped, preferred_element_type=jnp.float32)
            * score_scale
        )
        d_query_norm = rotate(d_query, cos_table, -sine_table)
        d_key_norm = rotate(d_key, cos_table, -sine_table)
        query_gain_part = jnp.sum(d_query_norm * query_hat, axis=(0, 1))
        key_gain_part = jnp.sum(d_key_norm * key_hat, axis=(0, 1))
        d_query_raw = rms_back(d_query_norm * query_gain_f, query_hat, query_scale)
        d_key_raw = rms_back(d_key_norm * key_gain_f, key_hat, key_scale)
        d_proj = jnp.concatenate(
            [
                d_query_raw.reshape(seq_len, query_cols),
                d_key_raw.reshape(seq_len, key_cols),
                d_value.reshape(seq_len, key_cols),
            ],
            axis=1,
        ).astype(jnp.bfloat16)
        grad_qkv = contract_rows(normed_full, d_proj)
        d_normed = lax.psum_scatter(
            row_back_product(d_proj, w_qkv), "narrow", scatter_dimension=0, tiled=True
        )
        attn_gain_part = jnp.sum(d_normed * hat_one, axis=0)
        in_grads.append(d_middle + rms_back(d_normed * attn_gain_f, hat_one, scale_one))
        grads_now = (grad_qkv, grad_both, grad_out, grad_down)
        small_now = (attn_gain_part, query_gain_part, key_gain_part, mlp_gain_part)
        if totals is None:
            totals = grads_now
            small_totals = small_now
        else:
            totals = tuple((running + extra for running, extra in zip(totals, grads_now)))
            small_totals = tuple(
                (running + extra for running, extra in zip(small_totals, small_now))
            )
    totals = (
        lax.psum_scatter(totals[0], "wide", scatter_dimension=0, tiled=True),
        lax.psum_scatter(totals[1], "wide", scatter_dimension=0, tiled=True),
        lax.psum_scatter(totals[2], "wide", scatter_dimension=1, tiled=True),
        lax.psum_scatter(totals[3], "wide", scatter_dimension=1, tiled=True),
    )
    small_sums = lax.psum(small_totals, ("wide", "narrow"))
    qkv_share, both_share, out_share, down_share = totals
    layer_out = jnp.stack(outputs_list)[:, None]
    in_grad = jnp.stack(in_grads)[:, None]
    return (
        layer_out,
        in_grad,
        small_sums[0],
        qkv_share[:, :query_cols],
        qkv_share[:, query_cols : query_cols + key_cols],
        qkv_share[:, query_cols + key_cols :],
        small_sums[1],
        small_sums[2],
        out_share,
        small_sums[3],
        both_share[:, :ff_cols],
        both_share[:, ff_cols:],
        down_share,
    )


def solution(mesh):
    in_specs = (
        P(None, "wide", "narrow", None),
        P(None, "wide", None),
        P(),
        P(None, "narrow"),
        P(None, "narrow"),
        P(None, "narrow"),
        P(),
        P(),
        P("narrow", None),
        P(),
        P(None, "narrow"),
        P(None, "narrow"),
        P("narrow", None),
        P(None, "wide", "narrow", None),
    )
    out_specs = (
        P(None, "wide", "narrow", None),
        P(None, "wide", "narrow", None),
        P(),
        P("wide", "narrow"),
        P("wide", "narrow"),
        P("wide", "narrow"),
        P(),
        P(),
        P("narrow", "wide"),
        P(),
        P("wide", "narrow"),
        P("wide", "narrow"),
        P("narrow", "wide"),
    )
    return jax.shard_map(local, mesh=mesh, in_specs=in_specs, out_specs=out_specs, check_vma=False)
```

profile of v0, /device:TPU:0, one launch (start us, length us, event | category | flops | bytes accessed | tf_op | source)
XLA Modules:
  0.0 1073.6 jit_solution(3452140487380955168)
XLA Ops:
  9.4 2.1 fusion.34
  18.1 3.2 constant_dynamic-update-slice_fusion.2
  23.4 18.8 %all-gather.11.cloned.1.call-done = bf16[256,2048]{1,0:T(8,128)(2,1)} async-done(((bf16[64,2048]{1,0:T(8,128)(2,1)}), bf16[256,2048]{1,0:T(8,128)(2,1)}) %all-gather.11.cloned.1.call-update) | async-done | bytes 1048592 | tf_op jit(solution)/shard_map/all_gather | solution.py:121
  42.3 3.8 fusion.110
  47.8 24.1 %all-gather.15.cloned.1.call-done = bf16[256,2048]{1,0:T(8,128)(2,1)} async-done(((bf16[64,2048]{1,0:T(8,128)(2,1)}), bf16[256,2048]{1,0:T(8,128)(2,1)}) %all-gather.15.cloned.1.call-update) | async-done | bytes 1048592 | tf_op jit(solution)/shard_map/all_gather | solution.py:121
  71.9 3.8 fusion.113
  82.0 2.2 multiply_multiply_fusion.1
  85.8 1.9 reshape.535
  87.7 2.0 multiply_reduce_fusion.15
  101.0 2.1 fusion.111
  112.0 2.1 fusion.114
  114.8 31.8 %reduce-scatter.13.cloned.1.call-done = f32[64,2048]{1,0:T(8,128)} async-done(((f32[256,2048]{1,0:T(8,128)}), f32[64,2048]{1,0:T(8,128)}) %reduce-scatter.13.cloned.1.call-update) | async-done | bytes 524304 | tf_op jit(solution)/shard_map/reduce_scatter | solution.py:149
  146.6 45.5 %reduce-scatter.17.cloned.1.call-done = f32[64,2048]{1,0:T(8,128)} async-done(((f32[256,2048]{1,0:T(8,128)}), f32[64,2048]{1,0:T(8,128)}) %reduce-scatter.17.cloned.1.call-update) | async-done | bytes 524304 | tf_op jit(solution)/shard_map/reduce_scatter | solution.py:149
  192.1 2.9 multiply_reduce_fusion.10
  196.7 1.9 fusion.107
  198.8 6.0 constant_dynamic-update-slice_fusion.4
  204.8 5.9 constant_dynamic-update-slice_fusion.3
  210.8 13.3 %all-gather.13.cloned.1.call-done = bf16[256,2048]{1,0:T(8,128)(2,1)} async-done(((bf16[64,2048]{1,0:T(8,128)(2,1)}), bf16[256,2048]{1,0:T(8,128)(2,1)}) %all-gather.13.cloned.1.call-update) | async-done | bytes 1048592 | tf_op jit(solution)/shard_map/all_gather | solution.py:156
  224.0 10.0 fusion.112
  234.0 19.5 %all-gather.23.cloned.1.call-done = bf16[1,1,256,2048]{3,2,1,0:T(8,128)(2,1)} async-done(((bf16[1,1,64,2048]{3,2,1,0:T(8,128)(2,1)}), bf16[1,1,256,2048]{3,2,1,0:T(8,128)(2,1)}) %all-gather.23.cloned.1.call-update) | async-done | bytes 1048592 | tf_op jit(solution)/shard_map/all_gather | solution.py:171
  253.5 7.2 multiply_convert_fusion.3
  261.9 9.4 fusion.21
  272.5 42.3 %reduce-scatter.21.cloned.1.call-done = f32[64,2048]{1,0:T(8,128)} async-done(((f32[256,2048]{1,0:T(8,128)}), f32[64,2048]{1,0:T(8,128)}) %reduce-scatter.21.cloned.1.call-update) | async-done | bytes 524304 | tf_op jit(solution)/shard_map/reduce_scatter | solution.py:178
  314.8 2.9 multiply_reduce_fusion.3
  318.9 26.2 %all-gather.17.cloned.1.call-done = bf16[256,2048]{1,0:T(8,128)(2,1)} async-done(((bf16[64,2048]{1,0:T(8,128)(2,1)}), bf16[256,2048]{1,0:T(8,128)(2,1)}) %all-gather.17.cloned.1.call-update) | async-done | bytes 1048592 | tf_op jit(solution)/shard_map/all_gather | solution.py:156
  345.1 10.0 fusion.115
  355.1 19.1 %all-gather.25.cloned.1.call-done = bf16[1,1,256,2048]{3,2,1,0:T(8,128)(2,1)} async-done(((bf16[1,1,64,2048]{3,2,1,0:T(8,128)(2,1)}), bf16[1,1,256,2048]{3,2,1,0:T(8,128)(2,1)}) %all-gather.25.cloned.1.call-update) | async-done | bytes 1048592 | tf_op jit(solution)/shard_map/all_gather | solution.py:171
  374.2 7.2 multiply_convert_fusion.1
  382.6 9.4 fusion.19
  392.1 5.8 convolution_convert_fusion
  399.1 36.4 %reduce-scatter.25.cloned.1.call-done = f32[64,2048]{1,0:T(8,128)} async-done(((f32[256,2048]{1,0:T(8,128)}), f32[64,2048]{1,0:T(8,128)}) %reduce-scatter.25.cloned.1.call-update) | async-done | bytes 524304 | tf_op jit(solution)/shard_map/reduce_scatter | solution.py:178
  435.5 2.0 multiply_reduce_fusion.2
  438.1 26.9 %reduce-scatter.19.cloned.1.call-done = bf16[64,2048]{1,0:T(8,128)(2,1)} async-done(((bf16[256,2048]{1,0:T(8,128)(2,1)}), bf16[64,2048]{1,0:T(8,128)(2,1)}) %reduce-scatter.19.cloned.1.call-update) | async-done | bytes 262160 | tf_op jit(solution)/shard_map/reduce_scatter | solution.py:163
  464.9 2.9 fusion.99
  473.6 21.0 %all-gather.19.cloned.1.call-done = bf16[256,2048]{1,0:T(8,128)(2,1)} async-done(((bf16[64,2048]{1,0:T(8,128)(2,1)}), bf16[256,2048]{1,0:T(8,128)(2,1)}) %all-gather.19.cloned.1.call-update) | async-done | bytes 1048592 | tf_op jit(solution)/shard_map/all_gather | solution.py:186
  494.6 2.7 convolution_convert_fusion.3
  497.3 1.8 copy.291
  499.1 2.3 fusion.10
  501.4 3.3 multiply_reduce_fusion.1
  504.7 19.0 %all-gather.21.cloned.1.call-done = bf16[256,2048]{1,0:T(8,128)(2,1)} async-done(((bf16[64,2048]{1,0:T(8,128)(2,1)}), bf16[256,2048]{1,0:T(8,128)(2,1)}) %all-gather.21.cloned.1.call-update) | async-done | bytes 1048592 | tf_op jit(solution)/shard_map/all_gather | solution.py:186
  523.7 2.7 convolution_convert_fusion.2
  537.8 2.4 multiply_reduce_fusion.13
  544.3 1.9 copy.285
  549.1 4.4 multiply_reduce_fusion.6
  556.5 4.8 fusion.76
  570.8 4.9 fusion.74
  575.8 5.7 convolution_convert_fusion.1
  581.6 2.3 fusion.75
  583.9 4.6 convolution_add_fusion.2
  589.7 11.6 %fusion.20 = f32[2048,3072]{1,0:T(8,128)} fusion(bf16[256,2048]{1,0:T(8,128)(2,1)S(1)} %copy-done.44, bf16[256,1536]{1,0:T(8,128)(2,1)} %copy-done.67, bf16[256,1536]{1,0:T(8,128)(2,1)} %copy-done.66), kind=kOutput, calls=%fused_computation.62 | convolution fusion | flops 3224371200 | bytes 27787264 | tf_op jit(solution)/shard_map/dot_general | solution.py:51
  601.3 16.9 %convolution_add_fusion = f32[2048,3072]{1,0:T(8,128)} fusion(f32[2048,3072]{1,0:T(8,128)} %fusion.20, bf16[256,2048]{1,0:T(8,128)(2,1)S(1)} %copy-done.40, bf16[256,1536]{1,0:T(8,128)(2,1)} %copy-done.64, bf16[256,1536]{1,0:T(8,128)(2,1)S(1)} %copy-done.63), kind=kOutput, calls=%fused_computation | convolution fusion | flops 3230662656 | bytes 52953088 | tf_op jit(solution)/shard_map/dot_general | solution.py:51
  620.3 2.8 convolution_add_fusion.3
  624.3 3.0 fusion.15
  627.3 6.5 convolution_add_fusion.1
  634.6 15.6 %reduce-scatter.27.cloned.1.call-done = f32[64,2048]{1,0:T(8,128)} async-done(((f32[256,2048]{1,0:T(8,128)}), f32[64,2048]{1,0:T(8,128)}) %reduce-scatter.27.cloned.1.call-update) | async-done | bytes 524304 | tf_op jit(solution)/shard_map/reduce_scatter | solution.py:220
  651.9 41.1 %all-reduce = (f32[2048]{0:T(1024)}, f32[128]{0:T(128)}, f32[128]{0:T(128)}, f32[2048]{0:T(1024)}) all-reduce(f32[2048]{0:T(1024)S(1)} %add.226, f32[128]{0:T(128)S(1)} %add.228, f32[128]{0:T(128)S(1)} %add.229, f32[2048]{0:T(1024)S(1)} %add.231), channel_id=1, replica_groups=mesh['wide'=8,'narrow'=4] {'wide','narrow'}, use_global_device_ids=true, to_apply=%region_38.39 | all-reduce | flops 4352 | bytes 34816 | tf_op jit(solution)/shard_map/psum | solution.py:241
  693.1 1.8 fusion.39
  697.4 56.1 %reduce-scatter.29.cloned.1.call-done = f32[256,1024]{1,0:T(8,128)} async-done(((f32[2048,1024]{1,0:T(8,128)}), f32[256,1024]{1,0:T(8,128)}) %reduce-scatter.29.cloned.1.call-update) | async-done | bytes 1048592 | tf_op jit(solution)/shard_map/reduce_scatter | solution.py:236
  753.5 1.9 slice.176
  755.4 2.0 fusion.102
  757.4 157.0 %reduce-scatter.33.cloned.1.call-done = f32[256,3072]{1,0:T(8,128)} async-done(((f32[2048,3072]{1,0:T(8,128)}), f32[256,3072]{1,0:T(8,128)}) %reduce-scatter.33.cloned.1.call-update) | async-done | bytes 3145744 | tf_op jit(solution)/shard_map/reduce_scatter | solution.py:237
  914.3 3.7 fusion.101
  918.1 51.9 %reduce-scatter.31.cloned.1.call-done = f32[512,256]{1,0:T(8,128)} async-done(((f32[512,2048]{1,0:T(8,128)}), f32[512,256]{1,0:T(8,128)}) %reduce-scatter.31.cloned.1.call-update) | async-done | bytes 524304 | tf_op jit(solution)/shard_map/reduce_scatter | solution.py:238
  970.0 96.3 %reduce-scatter.35.cloned.1.call-done = f32[1536,256]{1,0:T(8,128)} async-done(((f32[1536,2048]{1,0:T(8,128)}), f32[1536,256]{1,0:T(8,128)}) %reduce-scatter.35.cloned.1.call-update) | async-done | bytes 1572880 | tf_op jit(solution)/shard_map/reduce_scatter | solution.py:239
  (370 shorter events, 95.4 us)
Async XLA Ops:
  7.2 93.8 %copy-start = (bf16[512,2048]{1,0:T(8,128)(2,1)S(1)}, bf16[512,2048]{1,0:T(8,128)(2,1)}, u32[]{:S(2)}) copy-start(bf16[512,2048]{1,0:T(8,128)(2,1)} %param.22) | copy-start | bytes 6291460
  7.2 35.1 %all-gather.11.cloned.1.call-start = ((), (), s32[]{:S(2)}) async-start(), calls=%async_computation.12 | async-start | bytes 1310720 | tf_op jit(solution)/shard_map/all_gather | solution.py:121
  9.4 11.9 %copy-start.57 = (bf16[2048,256]{1,0:T(8,128)(2,1)S(1)}, bf16[2048,256]{1,0:T(8,128)(2,1)}, u32[]{:S(2)}) copy-start(bf16[2048,256]{1,0:T(8,128)(2,1)} %param.18) | copy-start | bytes 3145732
  11.5 60.4 %all-gather.15.cloned.1.call-start = ((), (), s32[]{:S(2)}) async-start(), calls=%async_computation.16 | async-start | bytes 1310720 | tf_op jit(solution)/shard_map/all_gather | solution.py:121
  12.2 134.4 %reduce-scatter.13.cloned.1.call-start = ((), (), s32[]{:S(2)}) async-start(), calls=%async_computation.13 | async-start | bytes 2621440 | tf_op jit(solution)/shard_map/reduce_scatter | solution.py:149
  13.0 69.0 %copy-start.98 = (f32[128]{0:T(128)}, f32[128]{0:T(128)S(1)}, u32[]{:S(2)}) copy-start(f32[128]{0:T(128)S(1)} %convert_element_type.147) | copy-start | bytes 1540
  15.6 76.6 %copy-start.102 = (f32[128]{0:T(128)}, f32[128]{0:T(128)S(1)}, u32[]{:S(2)}) copy-start(f32[128]{0:T(128)S(1)} %convert_element_type.145) | copy-start | bytes 1540
  46.0 31.4 %copy-start.20 = (f32[256,1024]{1,0:T(8,128)}, f32[256,1024]{1,0:T(8,128)S(1)}, u32[]{:S(2)}) copy-start(f32[256,1024]{1,0:T(8,128)S(1)} %fusion.110) | copy-start | bytes 3145732
  79.3 6.3 copy-start.8
  81.6 6.1 copy-start.10
  85.7 13.0 %copy-start.27 = (bf16[256,4,64]{2,0,1:T(8,128)(2,1)}, bf16[256,4,64]{2,0,1:T(8,128)(2,1)S(1)}, u32[]{:S(2)}) copy-start(bf16[256,4,64]{2,0,1:T(8,128)(2,1)S(1)} %copy.206) | copy-start | bytes 393220
  85.8 13.0 %copy-start.29 = (bf16[256,4,64]{2,0,1:T(8,128)(2,1)}, bf16[256,4,64]{2,0,1:T(8,128)(2,1)S(1)}, u32[]{:S(2)}) copy-start(bf16[256,4,64]{2,0,1:T(8,128)(2,1)S(1)} %copy.205) | copy-start | bytes 393220
  90.6 380.7 %copy-start.83 = (f32[256,2]{0,1:T(2,128)}, f32[256,2]{0,1:T(2,128)S(1)}, u32[]{:S(2)}) copy-start(f32[256,2]{0,1:T(2,128)S(1)} %add_rsqrt_fusion.3) | copy-start | bytes 6148
  103.1 89.0 %reduce-scatter.17.cloned.1.call-start = ((), (), s32[]{:S(2)}) async-start(), calls=%async_computation.17 | async-start | bytes 2621440 | tf_op jit(solution)/shard_map/reduce_scatter | solution.py:149
  103.2 5.3 copy-start.45
  114.1 110.0 %all-gather.13.cloned.1.call-start = ((), (), s32[]{:S(2)}) async-start(), calls=%async_computation.14 | async-start | bytes 1310720 | tf_op jit(solution)/shard_map/all_gather | solution.py:156
  196.6 56.9 %all-gather.23.cloned.1.call-start = ((), (), s32[]{:S(2)}) async-start(), calls=%async_computation.30 | async-start | bytes 1310720 | tf_op jit(solution)/shard_map/all_gather | solution.py:171
  198.6 116.2 %reduce-scatter.21.cloned.1.call-start = ((), (), s32[]{:S(2)}) async-start(), calls=%async_computation.20 | async-start | bytes 2621440 | tf_op jit(solution)/shard_map/reduce_scatter | solution.py:178
  271.2 73.9 %all-gather.17.cloned.1.call-start = ((), (), s32[]{:S(2)}) async-start(), calls=%async_computation.18 | async-start | bytes 1310720 | tf_op jit(solution)/shard_map/all_gather | solution.py:156
  317.7 56.5 %all-gather.25.cloned.1.call-start = ((), (), s32[]{:S(2)}) async-start(), calls=%async_computation.31 | async-start | bytes 1310720 | tf_op jit(solution)/shard_map/all_gather | solution.py:171
  318.4 117.1 %reduce-scatter.25.cloned.1.call-start = ((), (), s32[]{:S(2)}) async-start(), calls=%async_computation.23 | async-start | bytes 2621440 | tf_op jit(solution)/shard_map/reduce_scatter | solution.py:178
  392.0 72.9 %reduce-scatter.19.cloned.1.call-start = ((), (), s32[]{:S(2)}) async-start(), calls=%async_computation.19 | async-start | bytes 1310720 | tf_op jit(solution)/shard_map/reduce_scatter | solution.py:163
  397.9 96.7 %all-gather.19.cloned.1.call-start = ((), (), s32[]{:S(2)}) async-start(), calls=%async_computation.21 | async-start | bytes 1310720 | tf_op jit(solution)/shard_map/all_gather | solution.py:186
  467.9 55.8 %all-gather.21.cloned.1.call-start = ((), (), s32[]{:S(2)}) async-start(), calls=%async_computation.24 | async-start | bytes 1310720 | tf_op jit(solution)/shard_map/all_gather | solution.py:186
  468.6 166.0 %reduce-scatter.23.cloned.1.call-start = ((), (), s32[]{:S(2)}) async-start(), calls=%async_computation.22 | async-start | bytes 2621440 | tf_op jit(solution)/shard_map/reduce_scatter | solution.py:220
  532.3 5.4 copy-start.22
  532.3 5.4 copy-start.23
  532.4 5.4 copy-start.82
  532.8 8.2 copy-start.37
  536.6 5.6 copy-start.38
  543.1 6.0 copy-start.9
  543.1 6.0 copy-start.11
  547.6 5.9 copy-start.76
  549.0 5.2 copy-start.21
  549.1 5.8 copy-start.34
  549.1 6.5 copy-start.86
  556.5 5.9 copy-start.26
  561.3 7.1 copy-start.19
  561.3 7.1 copy-start.59
  561.3 8.6 copy-start.36
  561.3 88.9 %reduce-scatter.27.cloned.1.call-start = ((), (), s32[]{:S(2)}) async-start(), calls=%async_computation.25 | async-start | bytes 2621440 | tf_op jit(solution)/shard_map/reduce_scatter | solution.py:220
  575.7 117.3 %reduce-scatter.15.cloned.1.call-start = ((), (), s32[]{:S(2)}) async-start(), calls=%async_computation.15 | async-start | bytes 1310720 | tf_op jit(solution)/shard_map/reduce_scatter | solution.py:163
  575.8 5.8 copy-start.43
  575.8 5.8 copy-start.69
  581.5 172.0 %reduce-scatter.29.cloned.1.call-start = ((), (), s32[]{:S(2)}) async-start(), calls=%async_computation.26 | async-start | bytes 9437184 | tf_op jit(solution)/shard_map/reduce_scatter | solution.py:236
  588.5 12.8 %copy-start.40 = (bf16[256,2048]{1,0:T(8,128)(2,1)S(1)}, bf16[256,2048]{1,0:T(8,128)(2,1)}, u32[]{:S(2)}) copy-start(bf16[256,2048]{1,0:T(8,128)(2,1)} %all-gather.17.cloned.1.call-done) | copy-start | bytes 3145732
  588.5 12.8 %copy-start.63 = (bf16[256,1536]{1,0:T(8,128)(2,1)S(1)}, bf16[256,1536]{1,0:T(8,128)(2,1)}, u32[]{:S(2)}) copy-start(bf16[256,1536]{1,0:T(8,128)(2,1)} %copy-done.62) | copy-start | bytes 2359300
  588.5 325.8 %reduce-scatter.33.cloned.1.call-start = ((), (), s32[]{:S(2)}) async-start(), calls=%async_computation.28 | async-start | bytes 28311552 | tf_op jit(solution)/shard_map/reduce_scatter | solution.py:237
  618.3 351.7 %reduce-scatter.31.cloned.1.call-start = ((), (), s32[]{:S(2)}) async-start(), calls=%async_computation.27 | async-start | bytes 4718592 | tf_op jit(solution)/shard_map/reduce_scatter | solution.py:238
  623.1 443.2 %reduce-scatter.35.cloned.1.call-start = ((), (), s32[]{:S(2)}) async-start(), calls=%async_computation.29 | async-start | bytes 14155776 | tf_op jit(solution)/shard_map/reduce_scatter | solution.py:239
  633.8 16.4 %copy-start.4 = (bf16[2,1,64,2048]{3,2,1,0:T(8,128)(2,1)S(1)}, bf16[2,1,64,2048]{3,2,1,0:T(8,128)(2,1)}, u32[]{:S(2)}) copy-start(bf16[2,1,64,2048]{3,2,1,0:T(8,128)(2,1)} %param.14) | copy-start | bytes 1572868
  633.8 16.4 %copy-start.79 = (f32[2048]{0:T(1024)S(1)}, f32[2048]{0:T(1024)}, u32[]{:S(2)}) copy-start(f32[2048]{0:T(1024)} %copy-done.78) | copy-start | bytes 24580
  633.8 16.4 %copy-start.91 = (f32[64]{0:T(128)S(1)}, f32[64]{0:T(128)}, u32[]{:S(2)}) copy-start(f32[64]{0:T(128)} %copy-done.90) | copy-start | bytes 772
  633.8 16.4 %copy-start.93 = (f32[64]{0:T(128)S(1)}, f32[64]{0:T(128)}, u32[]{:S(2)}) copy-start(f32[64]{0:T(128)} %copy-done.92) | copy-start | bytes 772
  633.9 59.2 %copy-start.7 = (f32[64,2048]{1,0:T(8,128)S(1)}, f32[64,2048]{1,0:T(8,128)}, u32[]{:S(2)}) copy-start(f32[64,2048]{1,0:T(8,128)} %copy-done.6) | copy-start | bytes 1572868
  633.9 59.2 %copy-start.12 = (bf16[2,1,64,2048]{3,2,1,0:T(8,128)(2,1)S(1)}, bf16[2,1,64,2048]{3,2,1,0:T(8,128)(2,1)}, u32[]{:S(2)}) copy-start(bf16[2,1,64,2048]{3,2,1,0:T(8,128)(2,1)} %param.27) | copy-start | bytes 1572868
  633.9 59.2 %copy-start.15 = (f32[64,2048]{1,0:T(8,128)S(1)}, f32[64,2048]{1,0:T(8,128)}, u32[]{:S(2)}) copy-start(f32[64,2048]{1,0:T(8,128)} %reduce-scatter.21.cloned.1.call-done) | copy-start | bytes 1572868
  633.9 59.2 %copy-start.97 = (f32[64]{0:T(128)S(1)}, f32[64]{0:T(128)}, u32[]{:S(2)}) copy-start(f32[64]{0:T(128)} %copy-done.96) | copy-start | bytes 772
  633.9 59.2 %copy-start.101 = (f32[64]{0:T(128)S(1)}, f32[64]{0:T(128)}, u32[]{:S(2)}) copy-start(f32[64]{0:T(128)} %broadcast_multiply_fusion.7) | copy-start | bytes 772
  651.8 44.1 %copy-start.5 = (f32[64,2048]{1,0:T(8,128)S(1)}, f32[64,2048]{1,0:T(8,128)}, u32[]{:S(2)}) copy-start(f32[64,2048]{1,0:T(8,128)} %get-tuple-element.154) | copy-start | bytes 1572868
  651.9 44.1 %copy-start.14 = (f32[64,2048]{1,0:T(8,128)S(1)}, f32[64,2048]{1,0:T(8,128)}, u32[]{:S(2)}) copy-start(f32[64,2048]{1,0:T(8,128)} %reduce-scatter.25.cloned.1.call-done) | copy-start | bytes 1572868
  651.9 44.1 %copy-start.95 = (f32[64]{0:T(128)S(1)}, f32[64]{0:T(128)}, u32[]{:S(2)}) copy-start(f32[64]{0:T(128)} %add_rsqrt_fusion.4) | copy-start | bytes 772
  651.9 44.1 %copy-start.100 = (f32[64]{0:T(128)S(1)}, f32[64]{0:T(128)}, u32[]{:S(2)}) copy-start(f32[64]{0:T(128)} %broadcast_multiply_fusion.5) | copy-start | bytes 772
  755.4 311.0 %copy-start.1 = (bf16[512,2048]{1,0:T(8,128)(2,1)S(1)}, bf16[512,2048]{1,0:T(8,128)(2,1)}, u32[]{:S(2)}) copy-start(bf16[512,2048]{1,0:T(8,128)(2,1)} %param.22) | copy-start | bytes 6291460
  (60 other events, 140.3 us)
Sparse Core Ops, SparseCore 0:
  11.6 30.6 all-gather.10
  44.4 27.4 all-gather.14
  103.2 43.3 reduce-scatter.12
  148.8 43.1 reduce-scatter.16
  196.8 27.2 all-gather.12
  226.0 27.4 all-gather.22
  271.4 43.3 reduce-scatter.20
  317.8 27.2 all-gather.16
  346.8 27.4 all-gather.24
  392.1 43.3 reduce-scatter.24
  438.4 26.4 reduce-scatter.18
  468.0 26.5 all-gather.18
  496.3 27.4 all-gather.20
  561.4 43.3 reduce-scatter.22
  607.0 43.1 reduce-scatter.26
  653.0 27.1 reduce-scatter.14
  683.5 69.9 reduce-scatter.28
  757.4 156.8 reduce-scatter.32
  918.6 51.3 reduce-scatter.30
  973.9 92.3 reduce-scatter.34
where the time goes:
time: 1080 us; the launch traced here: 1070 us
  waiting for transfers between devices  723 us (67%)
  matrix products  156 us (14%)
  local copies, waits for them, and re-layouts  73.9 us (7%)
  other arithmetic  61.7 us (6%)
  blocking collectives  41.1 us (4%)
  between operations  16.1 us (1%)
    reduce_scatter x1, waiting for transfers between devices, local(): lax.psum_scatter(totals[1], 'wide', scatter_dimension=0, tiled=True)  157 us
    reduce_scatter x1, waiting for transfers between devices, local(): lax.psum_scatter(totals[3], 'wide', scatter_dimension=1, tiled=True)  96.3 us
    reduce_scatter x2, waiting for transfers between devices, local(): lax.psum_scatter(row_back_product(d_both, w_both), 'narrow', scatter_dime...  78.7 us
    reduce_scatter x2, waiting for transfers between devices, local(): lax.psum_scatter(row_product(attn_mix, w_out), 'narrow', scatter_dimensio...  77.3 us
    reduce_scatter x1, waiting for transfers between devices, local(): lax.psum_scatter(totals[0], 'wide', scatter_dimension=0, tiled=True)  56.1 us
    reduce_scatter x1, waiting for transfers between devices, local(): lax.psum_scatter(totals[2], 'wide', scatter_dimension=1, tiled=True)  51.9 us
    dot_general x8, matrix products, contract_rows(): lax.dot_general(left_side, right_side, (((0,), (0,)), ((), ())), preferre...  48.3 us
    dot_general x8, matrix products, contract_cols(): lax.dot_general(left_side, right_side, (((1,), (1,)), ((), ())), preferre...  48.1 us
  transfers between devices with their start and end apart: 20, of which 18 were waited for; matrix products, arithmetic and copies ran while one was open for 16% of the time, Pallas kernels for 0%

commit v1 on v0

--- a/solution.py
+++ b/solution.py
@@ -153,7 +153,23 @@
         scale_two = rms_scale(middle)
         hat_two = middle * scale_two
         normed_two = (hat_two * mlp_gain_f).astype(jnp.bfloat16)
-        normed_two_full = lax.all_gather(normed_two, "narrow", axis=0, tiled=True)
+        size, index, extent = (
+            lax.axis_size("narrow"),
+            lax.axis_index("narrow"),
+            normed_two.shape[0],
+        )
+        ahead = [(i, (i + 1) % size) for i in range(size)]
+        normed_two_full = jnp.zeros(
+            (*normed_two.shape[:0], size * extent, *normed_two.shape[0 + 1 :]), normed_two.dtype
+        )
+        current = normed_two
+        for step in range(size):
+            source_2 = (index - step) % size
+            normed_two_full = lax.dynamic_update_slice_in_dim(
+                normed_two_full, current, source_2 * extent, axis=0
+            )
+            if step < size - 1:
+                current = lax.ppermute(current, "narrow", ahead)
         gate_up = jnp.dot(normed_two_full, w_both, preferred_element_type=jnp.float32)
         gate_pre = gate_up[:, :ff_cols]
         up_proj = gate_up[:, ff_cols:]

time: 1080 us -> 1040 us (0.963)
  waiting for transfers between devices: 723 us -> 655 us
  starting transfers between devices: 2.07 us -> 22.4 us
    ppermute x0 -> x6, waiting for transfers between devices: none -> 49 us  [local(): current = lax.ppermute(current, 'narrow', ahead)]
    all_gather x2 -> x0, waiting for transfers between devices: 39.5 us -> none  [local(): normed_two_full = lax.all_gather(normed_two, 'narrow', axis=0, tiled=True)]
    all_gather x2, waiting for transfers between devices: 38.6 us -> 0.01 us  [local(): cot_full = lax.all_gather(cot_rows, 'narrow', axis=0, tiled=True)]
    reduce_scatter x2, waiting for transfers between devices: 78.7 us -> 43 us  [local(): lax.psum_scatter(row_back_product(d_both, w_both), 'narrow', scatter_dime...]
    ppermute x0 -> x6, starting transfers between devices: none -> 21 us  [local(): current = lax.ppermute(current, 'narrow', ahead)]
    unnamed x217 -> x223, local copies, waits for them, and re-layouts: 27.1 us -> 28.4 us
  transfers between devices with their start and end apart: 20 -> 24, of which waited for: 18 -> 19; matrix products, arithmetic and copies ran while one was open for 16% -> 20% of each run, Pallas kernels for 0% -> 0%
where the time goes in v1:
time: 1040 us; the launch traced here: 1030 us
  waiting for transfers between devices  655 us (63%)
  matrix products  156 us (15%)
  local copies, waits for them, and re-layouts  77.2 us (7%)
  other arithmetic  58.2 us (6%)
  blocking collectives  41.1 us (4%)
  starting transfers between devices  22.4 us (2%)
  between operations  16.2 us (2%)
    reduce_scatter x1, waiting for transfers between devices, local(): lax.psum_scatter(totals[1], 'wide', scatter_dimension=0, tiled=True)  157 us
    reduce_scatter x1, waiting for transfers between devices, local(): lax.psum_scatter(totals[3], 'wide', scatter_dimension=1, tiled=True)  96.3 us
    reduce_scatter x2, waiting for transfers between devices, local(): lax.psum_scatter(row_product(attn_mix, w_out), 'narrow', scatter_dimensio...  74.7 us
    reduce_scatter x1, waiting for transfers between devices, local(): lax.psum_scatter(totals[0], 'wide', scatter_dimension=0, tiled=True)  56.1 us
    reduce_scatter x1, waiting for transfers between devices, local(): lax.psum_scatter(totals[2], 'wide', scatter_dimension=1, tiled=True)  51.8 us
    ppermute x6, waiting for transfers between devices, local(): current = lax.ppermute(current, 'narrow', ahead)  49 us
    dot_general x8, matrix products, contract_rows(): lax.dot_general(left_side, right_side, (((0,), (0,)), ((), ())), preferre...  48.4 us
    dot_general x8, matrix products, contract_cols(): lax.dot_general(left_side, right_side, (((1,), (1,)), ((), ())), preferre...  48.2 us
  transfers between devices with their start and end apart: 24, of which 19 were waited for; matrix products, arithmetic and copies ran while one was open for 20% of the time, Pallas kernels for 0%

profile of v1, /device:TPU:0, one launch (start us, length us, event | category | flops | bytes accessed | tf_op | source)
XLA Modules:
  0.0 1025.8 jit_solution(3496927424790119982)
XLA Ops:
  9.4 2.1 fusion.34
  18.1 3.2 constant_dynamic-update-slice_fusion.2
  23.4 18.8 %all-gather.9.cloned.1.call-done = bf16[256,2048]{1,0:T(8,128)(2,1)} async-done(((bf16[64,2048]{1,0:T(8,128)(2,1)}), bf16[256,2048]{1,0:T(8,128)(2,1)}) %all-gather.9.cloned.1.call-update) | async-done | bytes 1048592 | tf_op jit(solution)/shard_map/all_gather | solution.py:121
  42.3 3.8 fusion.110
  47.8 24.1 %all-gather.11.cloned.1.call-done = bf16[256,2048]{1,0:T(8,128)(2,1)} async-done(((bf16[64,2048]{1,0:T(8,128)(2,1)}), bf16[256,2048]{1,0:T(8,128)(2,1)}) %all-gather.11.cloned.1.call-update) | async-done | bytes 1048592 | tf_op jit(solution)/shard_map/all_gather | solution.py:121
  71.9 3.8 fusion.113
  82.9 2.2 multiply_multiply_fusion.1
  91.1 1.9 fusion.72
  100.3 2.1 fusion.111
  111.3 2.1 fusion.114
  113.5 1.9 fusion.107
  116.7 29.2 %reduce-scatter.13.cloned.1.call-done = f32[64,2048]{1,0:T(8,128)} async-done(((f32[256,2048]{1,0:T(8,128)}), f32[64,2048]{1,0:T(8,128)}) %reduce-scatter.13.cloned.1.call-update) | async-done | bytes 524304 | tf_op jit(solution)/shard_map/reduce_scatter | solution.py:149
  145.9 45.5 %reduce-scatter.17.cloned.1.call-done = f32[64,2048]{1,0:T(8,128)} async-done(((f32[256,2048]{1,0:T(8,128)}), f32[64,2048]{1,0:T(8,128)}) %reduce-scatter.17.cloned.1.call-update) | async-done | bytes 524304 | tf_op jit(solution)/shard_map/reduce_scatter | solution.py:149
  191.4 2.9 multiply_reduce_fusion.10
  196.4 6.2 constant_dynamic-update-slice_fusion.4
  202.6 6.2 collective-permute-done
  210.5 3.2 constant_dynamic-update-slice_fusion.3
  214.8 9.3 collective-permute-done.1
  224.1 3.5 collective-permute-start.2
  231.0 3.3 collective-permute-done.2
  235.0 10.2 fusion.112
  245.3 7.2 multiply_convert_fusion.3
  253.7 9.4 fusion.21
  264.5 8.4 collective-permute-done.3
  272.8 6.6 collective-permute-start.4
  279.4 11.3 %collective-permute-done.4 = bf16[64,2048]{1,0:T(8,128)(2,1)S(1)} collective-permute-done((bf16[64,2048]{1,0:T(8,128)(2,1)S(1)}, bf16[64,2048]{1,0:T(8,128)(2,1)S(1)}, u32[]{:S(2)}, u32[]{:S(2)}) %collective-permute-start.4) | collective-permute-done | bytes 262176 | tf_op jit(solution)/shard_map/ppermute | solution.py:172
  290.7 9.1 collective-permute-start.5
  299.9 10.4 %collective-permute-done.5 = bf16[64,2048]{1,0:T(8,128)(2,1)S(1)} collective-permute-done((bf16[64,2048]{1,0:T(8,128)(2,1)S(1)}, bf16[64,2048]{1,0:T(8,128)(2,1)S(1)}, u32[]{:S(2)}, u32[]{:S(2)}) %collective-permute-start.5) | collective-permute-done | bytes 262176 | tf_op jit(solution)/shard_map/ppermute | solution.py:172
  311.3 9.7 fusion.115
  321.0 7.2 multiply_convert_fusion.1
  329.4 9.4 fusion.20
  338.8 5.8 convolution_convert_fusion
  344.7 43.0 %reduce-scatter.25.cloned.1.call-done = f32[64,2048]{1,0:T(8,128)} async-done(((f32[256,2048]{1,0:T(8,128)}), f32[64,2048]{1,0:T(8,128)}) %reduce-scatter.25.cloned.1.call-update) | async-done | bytes 524304 | tf_op jit(solution)/shard_map/reduce_scatter | solution.py:194
  387.7 2.5 multiply_reduce_fusion.3
  391.3 25.8 %reduce-scatter.19.cloned.1.call-done = bf16[64,2048]{1,0:T(8,128)(2,1)} async-done(((bf16[256,2048]{1,0:T(8,128)(2,1)}), bf16[64,2048]{1,0:T(8,128)(2,1)}) %reduce-scatter.19.cloned.1.call-update) | async-done | bytes 262160 | tf_op jit(solution)/shard_map/reduce_scatter | solution.py:179
  417.1 2.9 fusion.99
  425.6 21.1 %all-gather.13.cloned.1.call-done = bf16[256,2048]{1,0:T(8,128)(2,1)} async-done(((bf16[64,2048]{1,0:T(8,128)(2,1)}), bf16[256,2048]{1,0:T(8,128)(2,1)}) %all-gather.13.cloned.1.call-update) | async-done | bytes 1048592 | tf_op jit(solution)/shard_map/all_gather | solution.py:202
  446.8 2.7 convolution_convert_fusion.3
  451.2 2.3 fusion.10
  453.5 3.3 multiply_reduce_fusion.1
  456.8 19.1 %all-gather.15.cloned.1.call-done = bf16[256,2048]{1,0:T(8,128)(2,1)} async-done(((bf16[64,2048]{1,0:T(8,128)(2,1)}), bf16[256,2048]{1,0:T(8,128)(2,1)}) %all-gather.15.cloned.1.call-update) | async-done | bytes 1048592 | tf_op jit(solution)/shard_map/all_gather | solution.py:202
  475.9 2.7 convolution_convert_fusion.2
  489.9 2.4 multiply_reduce_fusion.13
  496.5 1.9 copy.285
  501.3 4.4 multiply_reduce_fusion.6
  508.6 4.8 fusion.76
  523.0 4.8 fusion.74
  528.0 5.7 convolution_convert_fusion.1
  533.8 2.3 fusion.75
  536.1 4.6 convolution_add_fusion.2
  541.9 11.6 %fusion.19 = f32[2048,3072]{1,0:T(8,128)} fusion(bf16[256,2048]{1,0:T(8,128)(2,1)S(1)} %copy-done.15, bf16[256,1536]{1,0:T(8,128)(2,1)} %copy-done.68, bf16[256,1536]{1,0:T(8,128)(2,1)} %copy-done.67), kind=kOutput, calls=%fused_computation.61 | convolution fusion | flops 3224371200 | bytes 27787264 | tf_op jit(solution)/shard_map/dot_general | solution.py:51
  553.5 16.9 %convolution_add_fusion = f32[2048,3072]{1,0:T(8,128)} fusion(f32[2048,3072]{1,0:T(8,128)} %fusion.19, bf16[256,2048]{1,0:T(8,128)(2,1)S(1)} %copy-done.13, bf16[256,1536]{1,0:T(8,128)(2,1)} %copy-done.65, bf16[256,1536]{1,0:T(8,128)(2,1)S(1)} %copy-done.64), kind=kOutput, calls=%fused_computation | convolution fusion | flops 3230662656 | bytes 52953088 | tf_op jit(solution)/shard_map/dot_general | solution.py:51
  572.5 2.8 convolution_add_fusion.3
  576.5 3.0 fusion.15
  579.5 6.5 convolution_add_fusion.1
  586.8 15.7 %reduce-scatter.27.cloned.1.call-done = f32[64,2048]{1,0:T(8,128)} async-done(((f32[256,2048]{1,0:T(8,128)}), f32[64,2048]{1,0:T(8,128)}) %reduce-scatter.27.cloned.1.call-update) | async-done | bytes 524304 | tf_op jit(solution)/shard_map/reduce_scatter | solution.py:236
  604.2 41.1 %all-reduce = (f32[2048]{0:T(1024)}, f32[128]{0:T(128)}, f32[128]{0:T(128)}, f32[2048]{0:T(1024)}) all-reduce(f32[2048]{0:T(1024)S(1)} %add.270, f32[128]{0:T(128)S(1)} %add.272, f32[128]{0:T(128)S(1)} %add.273, f32[2048]{0:T(1024)S(1)} %add.275), channel_id=1, replica_groups=mesh['wide'=8,'narrow'=4] {'wide','narrow'}, use_global_device_ids=true, to_apply=%region_38.39 | all-reduce | flops 4352 | bytes 34816 | tf_op jit(solution)/shard_map/psum | solution.py:257
  649.8 56.1 %reduce-scatter.29.cloned.1.call-done = f32[256,1024]{1,0:T(8,128)} async-done(((f32[2048,1024]{1,0:T(8,128)}), f32[256,1024]{1,0:T(8,128)}) %reduce-scatter.29.cloned.1.call-update) | async-done | bytes 1048592 | tf_op jit(solution)/shard_map/reduce_scatter | solution.py:252
  705.8 1.9 slice.176
  707.7 2.0 fusion.102
  709.7 156.9 %reduce-scatter.33.cloned.1.call-done = f32[256,3072]{1,0:T(8,128)} async-done(((f32[2048,3072]{1,0:T(8,128)}), f32[256,3072]{1,0:T(8,128)}) %reduce-scatter.33.cloned.1.call-update) | async-done | bytes 3145744 | tf_op jit(solution)/shard_map/reduce_scatter | solution.py:253
  866.6 3.7 fusion.101
  870.4 51.8 %reduce-scatter.31.cloned.1.call-done = f32[512,256]{1,0:T(8,128)} async-done(((f32[512,2048]{1,0:T(8,128)}), f32[512,256]{1,0:T(8,128)}) %reduce-scatter.31.cloned.1.call-update) | async-done | bytes 524304 | tf_op jit(solution)/shard_map/reduce_scatter | solution.py:254
  922.2 96.3 %reduce-scatter.35.cloned.1.call-done = f32[1536,256]{1,0:T(8,128)} async-done(((f32[1536,2048]{1,0:T(8,128)}), f32[1536,256]{1,0:T(8,128)}) %reduce-scatter.35.cloned.1.call-update) | async-done | bytes 1572880 | tf_op jit(solution)/shard_map/reduce_scatter | solution.py:255
  (391 shorter events, 107.1 us)
Async XLA Ops:
  7.2 93.1 %copy-start = (bf16[512,2048]{1,0:T(8,128)(2,1)S(1)}, bf16[512,2048]{1,0:T(8,128)(2,1)}, u32[]{:S(2)}) copy-start(bf16[512,2048]{1,0:T(8,128)(2,1)} %param.22) | copy-start | bytes 6291460
  7.2 35.1 %all-gather.9.cloned.1.call-start = ((), (), s32[]{:S(2)}) async-start(), calls=%async_computation.12 | async-start | bytes 1310720 | tf_op jit(solution)/shard_map/all_gather | solution.py:121
  9.4 11.9 %copy-start.58 = (bf16[2048,256]{1,0:T(8,128)(2,1)S(1)}, bf16[2048,256]{1,0:T(8,128)(2,1)}, u32[]{:S(2)}) copy-start(bf16[2048,256]{1,0:T(8,128)(2,1)} %param.18) | copy-start | bytes 3145732
  11.5 60.4 %all-gather.11.cloned.1.call-start = ((), (), s32[]{:S(2)}) async-start(), calls=%async_computation.15 | async-start | bytes 1310720 | tf_op jit(solution)/shard_map/all_gather | solution.py:121
  12.2 133.7 %reduce-scatter.13.cloned.1.call-start = ((), (), s32[]{:S(2)}) async-start(), calls=%async_computation.13 | async-start | bytes 2621440 | tf_op jit(solution)/shard_map/reduce_scatter | solution.py:149
  13.0 69.9 %copy-start.99 = (f32[128]{0:T(128)}, f32[128]{0:T(128)S(1)}, u32[]{:S(2)}) copy-start(f32[128]{0:T(128)S(1)} %convert_element_type.147) | copy-start | bytes 1540
  15.6 75.5 %copy-start.101 = (f32[128]{0:T(128)}, f32[128]{0:T(128)S(1)}, u32[]{:S(2)}) copy-start(f32[128]{0:T(128)S(1)} %convert_element_type.145) | copy-start | bytes 1540
  80.2 6.3 copy-start.8
  82.5 6.6 copy-start.10
  89.5 333.9 %copy-start.84 = (f32[256,2]{0,1:T(2,128)}, f32[256,2]{0,1:T(2,128)S(1)}, u32[]{:S(2)}) copy-start(f32[256,2]{0,1:T(2,128)S(1)} %add_rsqrt_fusion.3) | copy-start | bytes 6148
  102.4 89.0 %reduce-scatter.17.cloned.1.call-start = ((), (), s32[]{:S(2)}) async-start(), calls=%async_computation.16 | async-start | bytes 2621440 | tf_op jit(solution)/shard_map/reduce_scatter | solution.py:149
  113.4 131.9 %all-gather.17.cloned.1.call-start = ((), (), s32[]{:S(2)}) async-start(), calls=%async_computation.28 | async-start | bytes 1310720 | tf_op jit(solution)/shard_map/all_gather | solution.py:187
  115.3 205.7 %all-gather.19.cloned.1.call-start = ((), (), s32[]{:S(2)}) async-start(), calls=%async_computation.29 | async-start | bytes 1310720 | tf_op jit(solution)/shard_map/all_gather | solution.py:187
  115.9 228.8 %reduce-scatter.21.cloned.1.call-start = ((), (), s32[]{:S(2)}) async-start(), calls=%async_computation.18 | async-start | bytes 2621440 | tf_op jit(solution)/shard_map/reduce_scatter | solution.py:194
  196.2 14.3 %slice-start = ((s8[6291456]{0:T(1024)(128)(4,1)}), s8[4194304]{0:T(1024)(128)(4,1)S(1)}, s32[]{:S(2)}) async-start(s8[6291456]{0:T(1024)(128)(4,1)} %bitcast.336), calls=%async_computation.30 | async-start | bytes 8388608
  196.2 14.3 %slice-start.1 = ((s8[6291456]{0:T(1024)(128)(4,1)}), s8[2097152]{0:T(1024)(128)(4,1)S(1)}, s32[]{:S(2)}) async-start(s8[6291456]{0:T(1024)(128)(4,1)} %bitcast.336), calls=%async_computation.31 | async-start | bytes 4194304
  196.2 12.6 %collective-permute-start = (bf16[64,2048]{1,0:T(8,128)(2,1)S(1)}, bf16[64,2048]{1,0:T(8,128)(2,1)}, u32[]{:S(2)}, u32[]{:S(2)}) collective-permute-start(bf16[64,2048]{1,0:T(8,128)(2,1)S(1)} %get-tuple-element.101), channel_id=1, source_target_pairs={{0,1},{1,2},{2,3},{3,0},{4,5},{5,6},{6,7},{7,4},{8,9},{9,10},{10,1... | collective-permute-start | bytes 786440 | tf_op jit(solution)/shard_map/ppermute | solution.py:172
  208.8 15.3 %collective-permute-start.1 = (bf16[64,2048]{1,0:T(8,128)(2,1)}, bf16[64,2048]{1,0:T(8,128)(2,1)}, u32[]{:S(2)}, u32[]{:S(2)}) collective-permute-start(bf16[64,2048]{1,0:T(8,128)(2,1)} %collective-permute-done), channel_id=1, source_target_pairs={{0,1},{1,2},{2,3},{3,0},{4,5},{5,6},{6,7},{7,4},{8,9},{9,10},{10,1... | collective-permute-start | bytes 786440 | tf_op jit(solution)/shard_map/ppermute | solution.py:172
  224.1 10.2 collective-permute-start.2
  263.0 124.6 %reduce-scatter.25.cloned.1.call-start = ((), (), s32[]{:S(2)}) async-start(), calls=%async_computation.21 | async-start | bytes 2621440 | tf_op jit(solution)/shard_map/reduce_scatter | solution.py:194
  264.4 8.5 collective-permute-start.3
  272.8 17.9 %collective-permute-start.4 = (bf16[64,2048]{1,0:T(8,128)(2,1)S(1)}, bf16[64,2048]{1,0:T(8,128)(2,1)S(1)}, u32[]{:S(2)}, u32[]{:S(2)}) collective-permute-start(bf16[64,2048]{1,0:T(8,128)(2,1)S(1)} %collective-permute-done.3), channel_id=1, source_target_pairs={{0,1},{1,2},{2,3},{3,0},{4,5},{5,6},{6,7},{7,4},{8,9},{9,10},{10,1... | collective-permute-start | bytes 786440 | tf_op jit(solution)/shard_map/ppermute | solution.py:172
  290.7 19.5 %collective-permute-start.5 = (bf16[64,2048]{1,0:T(8,128)(2,1)S(1)}, bf16[64,2048]{1,0:T(8,128)(2,1)S(1)}, u32[]{:S(2)}, u32[]{:S(2)}) collective-permute-start(bf16[64,2048]{1,0:T(8,128)(2,1)S(1)} %collective-permute-done.4), channel_id=1, source_target_pairs={{0,1},{1,2},{2,3},{3,0},{4,5},{5,6},{6,7},{7,4},{8,9},{9,10},{10,1... | collective-permute-start | bytes 786440 | tf_op jit(solution)/shard_map/ppermute | solution.py:172
  338.8 78.3 %reduce-scatter.19.cloned.1.call-start = ((), (), s32[]{:S(2)}) async-start(), calls=%async_computation.17 | async-start | bytes 1310720 | tf_op jit(solution)/shard_map/reduce_scatter | solution.py:179
  344.6 102.1 %all-gather.13.cloned.1.call-start = ((), (), s32[]{:S(2)}) async-start(), calls=%async_computation.19 | async-start | bytes 1310720 | tf_op jit(solution)/shard_map/all_gather | solution.py:202
  420.0 55.8 %all-gather.15.cloned.1.call-start = ((), (), s32[]{:S(2)}) async-start(), calls=%async_computation.22 | async-start | bytes 1310720 | tf_op jit(solution)/shard_map/all_gather | solution.py:202
  420.8 166.1 %reduce-scatter.23.cloned.1.call-start = ((), (), s32[]{:S(2)}) async-start(), calls=%async_computation.20 | async-start | bytes 2621440 | tf_op jit(solution)/shard_map/reduce_scatter | solution.py:236
  484.5 5.4 copy-start.26
  484.5 5.4 copy-start.27
  484.9 8.2 copy-start.40
  488.8 5.7 copy-start.41
  495.3 6.0 copy-start.9
  495.3 6.0 copy-start.11
  499.8 5.9 copy-start.77
  501.3 5.8 copy-start.37
  501.3 6.5 copy-start.87
  508.6 5.9 copy-start.30
  513.4 7.1 copy-start.23
  513.4 7.1 copy-start.60
  513.5 8.6 copy-start.39
  513.5 89.0 %reduce-scatter.27.cloned.1.call-start = ((), (), s32[]{:S(2)}) async-start(), calls=%async_computation.23 | async-start | bytes 2621440 | tf_op jit(solution)/shard_map/reduce_scatter | solution.py:236
  527.9 117.5 %reduce-scatter.15.cloned.1.call-start = ((), (), s32[]{:S(2)}) async-start(), calls=%async_computation.14 | async-start | bytes 1310720 | tf_op jit(solution)/shard_map/reduce_scatter | solution.py:179
  527.9 5.8 copy-start.45
  527.9 5.8 copy-start.70
  533.7 172.1 %reduce-scatter.29.cloned.1.call-start = ((), (), s32[]{:S(2)}) async-start(), calls=%async_computation.24 | async-start | bytes 9437184 | tf_op jit(solution)/shard_map/reduce_scatter | solution.py:252
  540.7 12.8 %copy-start.13 = (bf16[256,2048]{1,0:T(8,128)(2,1)S(1)}, bf16[256,2048]{1,0:T(8,128)(2,1)}, u32[]{:S(2)}) copy-start(bf16[256,2048]{1,0:T(8,128)(2,1)} %constant_dynamic-update-slice_fusion.8) | copy-start | bytes 3145732
  540.7 12.8 %copy-start.64 = (bf16[256,1536]{1,0:T(8,128)(2,1)S(1)}, bf16[256,1536]{1,0:T(8,128)(2,1)}, u32[]{:S(2)}) copy-start(bf16[256,1536]{1,0:T(8,128)(2,1)} %copy-done.63) | copy-start | bytes 2359300
  540.7 325.9 %reduce-scatter.33.cloned.1.call-start = ((), (), s32[]{:S(2)}) async-start(), calls=%async_computation.26 | async-start | bytes 28311552 | tf_op jit(solution)/shard_map/reduce_scatter | solution.py:253
  570.5 351.7 %reduce-scatter.31.cloned.1.call-start = ((), (), s32[]{:S(2)}) async-start(), calls=%async_computation.25 | async-start | bytes 4718592 | tf_op jit(solution)/shard_map/reduce_scatter | solution.py:254
  575.3 443.2 %reduce-scatter.35.cloned.1.call-start = ((), (), s32[]{:S(2)}) async-start(), calls=%async_computation.27 | async-start | bytes 14155776 | tf_op jit(solution)/shard_map/reduce_scatter | solution.py:255
  586.0 16.5 %copy-start.7 = (bf16[2,1,64,2048]{3,2,1,0:T(8,128)(2,1)S(1)}, bf16[2,1,64,2048]{3,2,1,0:T(8,128)(2,1)}, u32[]{:S(2)}) copy-start(bf16[2,1,64,2048]{3,2,1,0:T(8,128)(2,1)} %param.14) | copy-start | bytes 1572868
  586.0 16.5 %copy-start.80 = (f32[2048]{0:T(1024)S(1)}, f32[2048]{0:T(1024)}, u32[]{:S(2)}) copy-start(f32[2048]{0:T(1024)} %copy-done.79) | copy-start | bytes 24580
  586.0 16.5 %copy-start.95 = (f32[64]{0:T(128)S(1)}, f32[64]{0:T(128)}, u32[]{:S(2)}) copy-start(f32[64]{0:T(128)} %copy-done.94) | copy-start | bytes 772
  586.0 16.5 %copy-start.97 = (f32[64]{0:T(128)S(1)}, f32[64]{0:T(128)}, u32[]{:S(2)}) copy-start(f32[64]{0:T(128)} %copy-done.96) | copy-start | bytes 772
  586.1 59.3 %copy-start.6 = (f32[64,2048]{1,0:T(8,128)S(1)}, f32[64,2048]{1,0:T(8,128)}, u32[]{:S(2)}) copy-start(f32[64,2048]{1,0:T(8,128)} %copy-done.5) | copy-start | bytes 1572868
  586.1 59.3 %copy-start.16 = (bf16[2,1,64,2048]{3,2,1,0:T(8,128)(2,1)S(1)}, bf16[2,1,64,2048]{3,2,1,0:T(8,128)(2,1)}, u32[]{:S(2)}) copy-start(bf16[2,1,64,2048]{3,2,1,0:T(8,128)(2,1)} %param.27) | copy-start | bytes 1572868
  586.1 59.3 %copy-start.18 = (f32[64,2048]{1,0:T(8,128)S(1)}, f32[64,2048]{1,0:T(8,128)}, u32[]{:S(2)}) copy-start(f32[64,2048]{1,0:T(8,128)} %reduce-scatter.21.cloned.1.call-done) | copy-start | bytes 1572868
  586.1 59.3 %copy-start.92 = (f32[64]{0:T(128)S(1)}, f32[64]{0:T(128)}, u32[]{:S(2)}) copy-start(f32[64]{0:T(128)} %copy-done.91) | copy-start | bytes 772
  586.1 59.3 %copy-start.103 = (f32[64]{0:T(128)S(1)}, f32[64]{0:T(128)}, u32[]{:S(2)}) copy-start(f32[64]{0:T(128)} %broadcast_multiply_fusion.7) | copy-start | bytes 772
  604.1 44.1 %copy-start.4 = (f32[64,2048]{1,0:T(8,128)S(1)}, f32[64,2048]{1,0:T(8,128)}, u32[]{:S(2)}) copy-start(f32[64,2048]{1,0:T(8,128)} %get-tuple-element.158) | copy-start | bytes 1572868
  604.2 44.1 %copy-start.19 = (f32[64,2048]{1,0:T(8,128)S(1)}, f32[64,2048]{1,0:T(8,128)}, u32[]{:S(2)}) copy-start(f32[64,2048]{1,0:T(8,128)} %reduce-scatter.25.cloned.1.call-done) | copy-start | bytes 1572868
  604.2 44.1 %copy-start.93 = (f32[64]{0:T(128)S(1)}, f32[64]{0:T(128)}, u32[]{:S(2)}) copy-start(f32[64]{0:T(128)} %add_rsqrt_fusion.4) | copy-start | bytes 772
  604.2 44.1 %copy-start.102 = (f32[64]{0:T(128)S(1)}, f32[64]{0:T(128)}, u32[]{:S(2)}) copy-start(f32[64]{0:T(128)} %broadcast_multiply_fusion.5) | copy-start | bytes 772
  707.7 310.8 %copy-start.1 = (bf16[512,2048]{1,0:T(8,128)(2,1)S(1)}, bf16[512,2048]{1,0:T(8,128)(2,1)}, u32[]{:S(2)}) copy-start(bf16[512,2048]{1,0:T(8,128)(2,1)} %param.22) | copy-start | bytes 6291460
  (67 other events, 171.0 us)
Sparse Core Ops, SparseCore 0:
  11.6 30.6 all-gather.8
  44.4 27.4 all-gather.10
  102.5 43.3 reduce-scatter.12
  148.2 43.1 reduce-scatter.16
  193.4 36.9 all-gather.16
  231.8 26.1 all-gather.18
  263.2 55.4 reduce-scatter.20
  338.9 48.7 reduce-scatter.24
  390.6 26.4 reduce-scatter.18
  420.2 26.5 all-gather.12
  448.4 27.4 all-gather.14
  513.6 43.3 reduce-scatter.22
  559.3 43.1 reduce-scatter.26
  605.3 27.1 reduce-scatter.14
  635.8 69.9 reduce-scatter.28
  709.7 156.8 reduce-scatter.32
  870.8 51.3 reduce-scatter.30
  926.1 92.3 reduce-scatter.34
